TPU v7x, 256 devices: a whole 4x4x8 slice. The times are simulated.
256 devices in a mesh: mod: 16 (over z, y_lo), pulse: 16 (over y_hi, x, core).
Axes of the slice: x: 4, y: 4 (y_hi: 2, y_lo: 2; y = y_hi * 2 + y_lo), z: 8, core: 2. Of those that a mesh axis runs over, the one named last changes fastest.
Arguments:
- raw_frames: bfloat16 [16, 16, 16, 128, 512], P('pulse', None, 'mod'), may hold values from -6 to 6
- gain_section: int32 [16, 16, 16, 16, 512], P('pulse', None, 'mod'), may hold values from 0 to 6560, as said below
- offset: float32 [16, 3, 128, 512], P('mod'), may hold values from -3 to 3
- gain_factor: float32 [16, 3, 128, 512], P('mod'), may hold values from 0.5 to 2
- row_map: bfloat16 [1024, 1024], replicated, as said below
- column_map: bfloat16 [1024, 1024], replicated
- reference_image: bfloat16 [1024, 1024], P(('mod', 'pulse')), may hold values from -6 to 6
- shifts: int32 [2, 16, 16, 64], P(None, 'pulse', 'mod'), may hold values from -24 to 24
Outputs:
- scores: float32 [16, 16, 64], P('pulse', 'mod')
- new_reference: float32 [1024, 1024], P(('mod', 'pulse'))
Inputs may be any that keep to these rules, and one draw needn't show every extreme that they name: `gain_section`: each word holds the gain sections 0, 1 or 2 of 8 consecutive pixel rows in base 3, row 8 p + k as the digit of 3 ** k. row_map and column_map are the identity plus a dense interpolation part.
All inputs are finite; a program needn't handle non-finite values.
Results may differ from a plain program's by a relative error of at most 0.0005.
The roundings to bfloat16 on the way count: a program that leaves them out, or rounds other values in their place, can miss the bound.
Values may be sent and summed in bfloat16 or wider, within the bound.
A program may use at most 128 MiB of HBM per device.

v0:
```python
import jax
import jax.numpy as jnp
from jax import lax
from jax.sharding import PartitionSpec as P

MR = 128
MC = 512
TS = 128
SH = 24
TILES = 64


prior_weight = 16.0


def unpack_section(packed):
    powers = jnp.array([1, 3, 9, 27, 81, 243, 729, 2187], dtype=jnp.int32)
    section = jnp.remainder(jnp.floor_divide(packed[..., :, None, :], powers[:, None]), 3)
    return section.reshape(packed.shape[:-2] + (packed.shape[-2] * 8, packed.shape[-1]))


def calibrate(raw_frames, gain_section, offset, gain_factor):
    dark_level = jnp.where(
        gain_section == 0, offset[:, 0], jnp.where(gain_section == 1, offset[:, 1], offset[:, 2])
    )
    factor = jnp.where(
        gain_section == 0,
        gain_factor[:, 0],
        jnp.where(gain_section == 1, gain_factor[:, 1], gain_factor[:, 2]),
    )
    return ((raw_frames.astype(jnp.float32) - dark_level) * factor).astype(jnp.bfloat16)


def assemble(modules_now):
    quadrants = modules_now.reshape(2, 2, 4, MR, MC)
    return quadrants.transpose(0, 2, 3, 1, 4).reshape(8 * MR, 2 * MC)


def frame_image(modules_now, row_map, column_map):
    assembled = assemble(modules_now)
    row_mapped = jnp.dot(row_map, assembled, preferred_element_type=jnp.float32).astype(
        jnp.bfloat16
    )
    return jnp.dot(row_mapped, column_map, preferred_element_type=jnp.float32).astype(jnp.bfloat16)


def track_tiles(lab_image, ref_padded, shift_rows, shift_cols, splat_map, cover_map):
    tiles_across = lab_image.shape[1] // TS
    tiles_count = lab_image.shape[0] // TS * tiles_across

    def tile_step(index, carried):
        splat_map, cover_map, scores = carried
        index = jnp.asarray(index).astype(jnp.int32)
        row_start = index // tiles_across * TS
        col_start = index % tiles_across * TS
        top_edge = row_start + shift_rows[index] + SH
        left_edge = col_start + shift_cols[index] + SH
        frame_tile = lax.dynamic_slice(lab_image, (row_start, col_start), (TS, TS)).astype(
            jnp.float32
        )
        window = lax.dynamic_slice(ref_padded, (top_edge, left_edge), (TS, TS)).astype(jnp.float32)
        score_value = jnp.sum(frame_tile * window) / TS
        weight = jax.nn.sigmoid(score_value)
        current = lax.dynamic_slice(splat_map, (top_edge, left_edge), (TS, TS))
        splat_map = lax.dynamic_update_slice(
            splat_map, current + weight * frame_tile, (top_edge, left_edge)
        )
        scores = scores.at[index].set(score_value)
        return (splat_map, cover_map, scores)

    start = (splat_map, cover_map, jnp.zeros((tiles_count,), jnp.float32))
    return lax.fori_loop(0, tiles_count, tile_step, start)


def reduce_single(splat_map):
    return lax.psum_scatter(splat_map, ("mod", "pulse"), scatter_dimension=0, tiled=True)


def recount(scores, shift_rows, shift_cols, height, width):
    weights = jax.nn.sigmoid(scores)
    all_weights, all_rows, all_cols = (
        lax.all_gather(weights, ("mod", "pulse"), axis=0, tiled=True),
        lax.all_gather(shift_rows.astype(jnp.float32), ("mod", "pulse"), axis=0, tiled=True),
        lax.all_gather(shift_cols.astype(jnp.float32), ("mod", "pulse"), axis=0, tiled=True),
    )
    tiles_across = width // TS
    tile_index = jnp.arange(TILES)
    base_rows = (tile_index // tiles_across * TS).astype(jnp.float32)
    base_cols = (tile_index % tiles_across * TS).astype(jnp.float32)
    group_size = 32
    block_count = all_weights.shape[0] // group_size
    block_width = group_size * TILES
    weight_blocks = all_weights.reshape(block_count, block_width)
    top_blocks = (all_rows + base_rows[None, :]).reshape(block_count, block_width)
    left_blocks = (all_cols + base_cols[None, :]).reshape(block_count, block_width)
    row_count = height // (lax.axis_size("mod") * lax.axis_size("pulse"))
    owner_index = lax.axis_index("mod") * lax.axis_size("pulse") + lax.axis_index("pulse")
    owner_rows = (owner_index * row_count + jnp.arange(row_count)).astype(jnp.float32)
    all_columns = jnp.arange(width).astype(jnp.float32)

    def add_block(running, block):
        weight_now, top_now, left_now = block
        row_hit = (
            (owner_rows[:, None] >= top_now[None, :])
            & (owner_rows[:, None] < top_now[None, :] + TS)
        ).astype(jnp.float32)
        col_hit = (
            (all_columns[None, :] >= left_now[:, None])
            & (all_columns[None, :] < left_now[:, None] + TS)
        ).astype(jnp.float32)
        product = jnp.dot(
            row_hit * weight_now[None, :],
            col_hit,
            precision=lax.Precision.HIGHEST,
            preferred_element_type=jnp.float32,
        )
        return (running + product, None)

    empty = jnp.zeros((row_count, width), jnp.float32)
    return lax.scan(add_block, empty, (weight_blocks, top_blocks, left_blocks))[0]


def per_device(
    raw_frames, gain_section, offset, gain_factor, row_map, column_map, reference_image, shifts
):
    calibrated = calibrate(raw_frames, unpack_section(gain_section), offset, gain_factor)
    regrouped = lax.all_to_all(calibrated, "mod", split_axis=1, concat_axis=2, tiled=True)
    whole_reference = lax.all_gather(reference_image, ("mod", "pulse"), axis=0, tiled=True)
    height = 8 * MR
    width = 2 * MC
    ref_padded = jnp.pad(whole_reference, SH)
    empty = jnp.zeros((height + 2 * SH, width + 2 * SH), jnp.float32)
    frames = regrouped[0]
    shift_rows = shifts[0, 0]
    shift_cols = shifts[1, 0]

    def per_frame(carried, inputs):
        modules_now, rows_now, cols_now = inputs
        lab_image = frame_image(modules_now, row_map, column_map)
        splat_map, cover_map, scores = track_tiles(
            lab_image, ref_padded, rows_now, cols_now, carried[0], carried[1]
        )
        return ((splat_map, cover_map), scores)

    (splat_map, cover_map), scores = lax.scan(
        per_frame, (empty, empty), (frames, shift_rows, shift_cols)
    )
    splat_map = splat_map[SH : SH + height, SH : SH + width]
    owned_splat = reduce_single(splat_map)
    owned_cover = recount(scores, shift_rows, shift_cols, height, width)
    new_reference = (owned_splat + prior_weight * reference_image.astype(jnp.float32)) / (
        owned_cover + prior_weight
    )
    return (scores.reshape(1, scores.shape[0], scores.shape[1]), new_reference)


def solution(mesh):
    return jax.shard_map(
        per_device,
        mesh=mesh,
        in_specs=(
            P("pulse", None, "mod", None, None),
            P("pulse", None, "mod", None, None),
            P("mod", None, None, None),
            P("mod", None, None, None),
            P(),
            P(),
            P(("mod", "pulse"), None),
            P(None, "pulse", "mod", None),
        ),
        out_specs=(P("pulse", "mod", None), P(("mod", "pulse"), None)),
        check_vma=False,
    )
```

profile of v0, /device:TPU:1, one launch (start us, length us, event | category | flops | bytes accessed | tf_op | source)
XLA Modules:
  0.0 1815.8 jit_solution(10373691381890550767)
XLA Ops:
  11.3 46.8 %multiply_convert_fusion = bf16[1,16,1,128,512]{4,3,2,0,1:T(8,128)(2,1)} fusion(bf16[1,16,1,128,512]{4,3,2,1,0:T(8,128)(2,1)S(1)} %copy-done.1, f32[128,512]{1,0:T(8,128)S(1)} %get-tuple-element.391, f32[128,512]{1,0:T(8,128)S(1)} %get-tuple-element.392, f32[128,512]{1,0:T(8,128)S(1)} %get-tuple-element.390, f32[128,512]{1,0:T(8,128)S(1)} %get-tuple-element.398, ...), kind=kLoop, calls=%fused_computation.36 | loop fusion | flops 23068672 | bytes 6423040 | tf_op jit(solution)/shard_map/convert_element_type | solution.py:31
  58.1 10.2 all-to-all-start
  69.3 47.6 %all-to-all-done = bf16[1,16,1,128,512]{4,3,2,0,1:T(8,128)(2,1)} async-done(((bf16[1,16,1,128,512]{4,3,2,0,1:T(8,128)(2,1)}), bf16[1,16,1,128,512]{4,3,2,0,1:T(8,128)(2,1)}, u32[]{:S(2)}, u32[]{:S(2)}) %all-to-all-start) | async-done | bytes 2097184 | tf_op jit(solution)/shard_map/all_to_all | solution.py:127
  117.0 3.8 copy.13
  122.6 8.2 fusion.26
  130.8 360.6 %all-gather.6.cloned.1.call-done = bf16[256,4,1024]{2,1,0:T(4,128)(2,1)} async-done(((bf16[1,4,1024]{2,1,0:T(4,128)(2,1)}), bf16[256,4,1024]{2,1,0:T(4,128)(2,1)}) %all-gather.6.cloned.1.call-update) | async-done | bytes 2097168 | tf_op jit(solution)/shard_map/all_gather | solution.py:128
  491.5 4.0 reshape.340
  495.4 4.2 pad.8
  502.2 588.9 %while.40 = (s32[]{:T(128)}, f32[1072,1072]{1,0:T(8,128)}, f32[64]{0:T(128)S(1)}, s32[64]{0:T(128)S(1)}, s32[64]{0:T(128)S(1)}, /*index=5*/bf16[1024,1024]{1,0:T...) while((s32[]{:T(128)}, f32[1072,1072]{1,0:T(8,128)}, ...), condition=%wide.region_2.3_spmd, body=%wide.region_0.2_spmd.sunk | while | flops 114727 | bytes 361614 | solution.py:72
  508.0 3.2 dynamic_update_slice.15
  517.2 3.2 dynamic_update_slice.15
  535.5 3.2 dynamic_update_slice.15
  544.7 3.3 dynamic_update_slice.15
  563.2 3.2 dynamic_update_slice.15
  572.4 3.3 dynamic_update_slice.15
  581.7 3.2 dynamic_update_slice.15
  590.9 3.2 dynamic_update_slice.15
  600.1 3.2 dynamic_update_slice.15
  609.3 3.3 dynamic_update_slice.15
  618.6 3.2 dynamic_update_slice.15
  627.8 3.3 dynamic_update_slice.15
  637.0 3.2 dynamic_update_slice.15
  646.3 3.2 dynamic_update_slice.15
  664.5 3.2 dynamic_update_slice.15
  673.7 3.2 dynamic_update_slice.15
  682.9 3.2 dynamic_update_slice.15
  692.2 3.2 dynamic_update_slice.15
  701.4 3.2 dynamic_update_slice.15
  710.6 3.3 dynamic_update_slice.15
  719.9 3.2 dynamic_update_slice.15
  729.1 3.2 dynamic_update_slice.15
  738.3 3.2 dynamic_update_slice.15
  747.5 3.2 dynamic_update_slice.15
  756.7 3.2 dynamic_update_slice.15
  765.9 3.3 dynamic_update_slice.15
  775.2 3.2 dynamic_update_slice.15
  784.4 3.3 dynamic_update_slice.15
  793.7 3.3 dynamic_update_slice.15
  802.9 3.2 dynamic_update_slice.15
  812.2 3.2 dynamic_update_slice.15
  821.4 3.2 dynamic_update_slice.15
  839.8 3.2 dynamic_update_slice.15
  849.0 3.3 dynamic_update_slice.15
  858.3 3.2 dynamic_update_slice.15
  867.5 3.3 dynamic_update_slice.15
  876.8 3.2 dynamic_update_slice.15
  895.2 3.2 dynamic_update_slice.15
  904.4 3.2 dynamic_update_slice.15
  913.7 3.2 dynamic_update_slice.15
  922.9 3.2 dynamic_update_slice.15
  932.1 3.2 dynamic_update_slice.15
  941.3 3.2 dynamic_update_slice.15
  950.5 3.2 dynamic_update_slice.15
  959.7 3.2 dynamic_update_slice.15
  969.0 3.2 dynamic_update_slice.15
  978.2 3.2 dynamic_update_slice.15
  987.4 3.3 dynamic_update_slice.15
  996.7 3.2 dynamic_update_slice.15
  1005.9 3.2 dynamic_update_slice.15
  1015.1 3.3 dynamic_update_slice.15
  1091.1 5.5 slice.52
  1097.4 343.7 %all-gather = f32[256,1,1,64]{3,2,1,0:T(1,128)S(1)} all-gather(f32[1,1,1,64]{3,2,1,0:T(1,128)S(1)} %get-tuple-element.394), channel_id=2, replica_groups=mesh['mod'=16,'pulse'=16] {'mod','pulse'}, dimensions={0}, use_global_device_ids=true | all-gather | bytes 65792 | tf_op jit(solution)/shard_map/all_gather | solution.py:83
  1441.2 340.2 %all-gather.2 = f32[256,1,1,64]{3,2,1,0:T(1,128)S(1)} all-gather(f32[1,1,1,64]{3,2,1,0:T(1,128)S(1)} %get-tuple-element.393), channel_id=4, replica_groups=mesh['mod'=16,'pulse'=16] {'mod','pulse'}, dimensions={0}, use_global_device_ids=true | all-gather | bytes 65792 | tf_op jit(solution)/shard_map/all_gather | solution.py:84
  1782.4 25.1 %while.41 = (s32[]{:T(128)}, f32[4,1024]{1,0:T(4,128)S(1)}, f32[8,2048]{1,0:T(8,128)S(1)}, f32[8,2048]{1,0:T(8,128)S(1)}, f32[8,2048]{1,0:T(8,128)S(1)}, /*index=5*/s32[]{:T(128)}, s32[]{:T(128)}, s32[]{:T(128)}) while((s32[]{:T(128)}, f32[4,1024]{1,0:T(4,128)S(1)}, f32[8,2048]{1,0:T(8,128)S(1)}, ...), condition=%wide.region_5.6_spmd.clone.clone, body=%wide.region_4.5_spmd.clone.clone.sunk | while | flops 107000840 | bytes 155787 | solution.py:120
  (417 shorter events, 330.0 us)
Async XLA Ops:
  7.2 115.4 %copy-start = (bf16[1024,1024]{1,0:T(8,128)(2,1)S(1)}, bf16[1024,1024]{1,0:T(8,128)(2,1)}, u32[]{:S(2)}) copy-start(bf16[1024,1024]{1,0:T(8,128)(2,1)} %param.20) | copy-start | bytes 6291460
  9.3 2.1 copy-start.1
  11.3 58.0 %copy-start.5 = (s32[2,1,1,64]{3,2,1,0:T(1,128)S(1)}, s32[2,1,1,64]{3,2,1,0:T(1,128)}, u32[]{:S(2)}) copy-start(s32[2,1,1,64]{3,2,1,0:T(1,128)} %param.22) | copy-start | bytes 1540
  58.1 58.8 %all-to-all-start = ((bf16[1,16,1,128,512]{4,3,2,0,1:T(8,128)(2,1)}), bf16[1,16,1,128,512]{4,3,2,0,1:T(8,128)(2,1)}, u32[]{:S(2)}, u32[]{:S(2)}) async-start(bf16[1,16,1,128,512]{4,3,2,0,1:T(8,128)(2,1)} %multiply_convert_fusion), calls=%async_computation | async-start | bytes 4194304 | tf_op jit(solution)/shard_map/all_to_all | solution.py:127
  68.3 423.1 %all-gather.6.cloned.1.call-start = ((), (), s32[]{:S(2)}) async-start(), calls=%async_computation.1 | async-start | bytes 2105344 | tf_op jit(solution)/shard_map/all_gather | solution.py:128
  69.1 1712.5 %all-reduce.6.cloned.1.call-start = ((), (), s32[]{:S(2)}) async-start(), calls=%async_computation.2 | async-start | bytes 8519680
  1091.1 5.5 copy-start.4
  1096.7 0.6 copy-start.2
  1782.4 25.2 %copy-start.3 = (bf16[4,1024]{1,0:T(4,128)(2,1)S(1)}, bf16[4,1024]{1,0:T(4,128)(2,1)}, u32[]{:S(2)}) copy-start(bf16[4,1024]{1,0:T(4,128)(2,1)} %param.21) | copy-start | bytes 24580
Sparse Core Ops, SparseCore 0:
  71.0 420.3 all-gather.5
  1097.5 271.4 all-reduce.5
where the time goes:
time: 1830 us; the launch traced here: 1820 us
  blocking collectives  684 us (37%)
  waiting for transfers between devices  409 us (22%)
  local copies, waits for them, and re-layouts  307 us (17%)
  other arithmetic  227 us (12%)
  loops' own time  132 us (7%)
  matrix products  32.6 us (2%)
    all_gather x1, waiting for transfers between devices, per_device(): lax.all_gather(reference_image, ('mod', 'pulse'), axis=0, tiled=True)  361 us
    all_gather x1, blocking collectives, recount(): lax.all_gather(shift_rows.astype(jnp.float32), ('mod', 'pulse'), axis=0,...  344 us
    all_gather x1, blocking collectives, recount(): lax.all_gather(shift_cols.astype(jnp.float32), ('mod', 'pulse'), axis=0,...  340 us
    dynamic_update_slice x64, local copies, waits for them, and re-layouts, tile_step(): lax.dynamic_update_slice(splat_map, current + weight * frame_tile, (top_e...  205 us
    another operation x1, loops' own time, track_tiles(): return lax.fori_loop(0, tiles_count, tile_step, start)  131 us
    reduce_sum x64, other arithmetic, tile_step(): score_value = jnp.sum(frame_tile * window) / TS  102 us
    add x64, other arithmetic, tile_step(): current + weight * frame_tile  65 us
    all_to_all x1, waiting for transfers between devices, per_device(): lax.all_to_all(calibrated, 'mod', split_axis=1, concat_axis=2, tiled=True)  47.6 us
  transfers between devices with their start and end apart: 3, of which 2 were waited for; matrix products, arithmetic and copies ran while one was open for 1% of the time, Pallas kernels for 0%

commit v1 on v0

v1 whole, which is shorter than its diff:
```python
import functools

import jax
import jax.numpy as jnp
from jax import lax
from jax.experimental import pallas as pl
from jax.experimental.pallas import tpu as pltpu
from jax.sharding import PartitionSpec as P

MR = 128
MC = 512
TS = 128
SH = 24
TILES = 64
IMG = 1024
PRIOR = 16.0
MESH = pl.DeviceIdType.MESH
F32 = jnp.float32
BF16 = jnp.bfloat16
I32 = jnp.int32


def coords():
    mod = lax.axis_index("mod")
    pulse = lax.axis_index("pulse")
    z = mod // 2
    y = (pulse // 8) * 2 + mod % 2
    x = (pulse // 2) % 4
    core = pulse % 2
    return z, y, x, core


def device(z, y, x, core):
    return (z * 2 + y % 2, (y // 2) * 8 + x * 2 + core)


def remote(src, dst, send_sem, recv_sem, target):
    return pltpu.make_async_remote_copy(
        src_ref=src,
        dst_ref=dst,
        send_sem=send_sem,
        recv_sem=recv_sem,
        device_id=target,
        device_id_type=MESH,
    )


def greet(targets):
    barrier = pltpu.get_barrier_semaphore()
    for target in targets:
        pl.semaphore_signal(barrier, inc=1, device_id=target, device_id_type=MESH)
    pl.semaphore_wait(barrier, len(targets))


VM = pl.BlockSpec(memory_space=pltpu.VMEM)
ANY = pl.BlockSpec(memory_space=pl.ANY)


def calibrate_kernel(raw_ref, gain_ref, off_ref, fac_ref, out_ref):
    k = lax.broadcasted_iota(I32, (8, MC), 0)
    inv = jnp.full((8, MC), 1.0, F32)
    for step in range(1, 8):
        inv = jnp.where(k == step, jnp.float32(1.0 / 3.0**step), inv)
    inv_next = inv * jnp.float32(1.0 / 3.0)
    for p in range(MR // 8):
        rows = pl.ds(8 * p, 8)
        packed = gain_ref[0, pl.ds(p, 1), :].astype(F32) + 0.5
        packed = jnp.broadcast_to(packed, (8, MC))
        digit = jnp.floor(packed * inv) - 3.0 * jnp.floor(packed * inv_next)
        low = digit < 0.5
        mid = digit < 1.5
        dark = jnp.where(low, off_ref[0, rows, :], jnp.where(mid, off_ref[1, rows, :], off_ref[2, rows, :]))
        fac = jnp.where(low, fac_ref[0, rows, :], jnp.where(mid, fac_ref[1, rows, :], fac_ref[2, rows, :]))
        value = (raw_ref[0, rows, :].astype(F32) - dark) * fac
        out_ref[0, rows, :] = value.astype(BF16)


def calibrate(raw, gain, off, fac):
    frames = raw.shape[0]
    return pl.pallas_call(
        calibrate_kernel,
        grid=(frames,),
        in_specs=[
            pl.BlockSpec((1, MR, MC), lambda f: (f, 0, 0)),
            pl.BlockSpec((1, MR // 8, MC), lambda f: (f, 0, 0)),
            pl.BlockSpec((3, MR, MC), lambda f: (0, 0, 0)),
            pl.BlockSpec((3, MR, MC), lambda f: (0, 0, 0)),
        ],
        out_specs=pl.BlockSpec((1, MR, MC), lambda f: (f, 0, 0)),
        out_shape=jax.ShapeDtypeStruct((frames, MR, MC), BF16),
        name="calibrate",
    )(raw, gain, off, fac)


def exchange_kernel(
    cal_ref, ref_ref, sh_ref,
    img_ref, rf_ref, shc_ref, sha_ref,
    ra, rtmp, rsl, rb, rc, srow, srow_in, sx, sy,
    a_send, a_recv, r_send, r_recv, z_send, z_recv, y_send, y_recv,
    c_send, c_recv, x_send, x_recv, s_send, s_recv, l_sem,
):
    z, y, x, core = coords()
    mod = lax.axis_index("mod")
    pulse = lax.axis_index("pulse")
    peers = [((mod + i) % 16, pulse) for i in range(1, 16)]
    plane = [device(z, y, (x + (i // 2)) % 4, (core + i) % 2) for i in range(1, 8)]
    greet(peers + plane + [device(z, (y + 2) % 4, x, core), device(z, (y + 3 - 2 * (y % 2)) % 4, x, core)])

    quad = mod // 4
    row0 = pl.multiple_of((quad // 2) * 512 + (mod % 4) * MR, MR)
    col0 = pl.multiple_of((quad % 2) * MC, MC)
    spot = img_ref.at[pl.ds(row0, MR), pl.ds(col0, MC)]

    j = x * 2 + core
    first = []
    for i in range(1, 8):
        copy = remote(ref_ref, ra.at[j], r_send.at[i - 1], r_recv.at[i - 1], plane[i - 1])
        copy.start()
        first.append(copy)
    own_ref = pltpu.make_async_copy(ref_ref, ra.at[j], l_sem.at[0])
    own_ref.start()

    lane = lax.broadcasted_iota(I32, (2, 128), 1)
    srow[:, 0:64] = sh_ref[...]
    srow[:, 64:128] = sh_ref[...]
    srow[...] = jnp.where(lane // 64 == core, srow[...], 0)
    partner = device(z, y, x, 1 - core)
    s0 = remote(srow, srow_in, s_send.at[0], s_recv.at[0], partner)
    s0.start()

    big = []
    for i in range(1, 16):
        copy = remote(cal_ref.at[(mod + i) % 16], spot, a_send.at[i - 1], a_recv.at[i - 1], peers[i - 1])
        copy.start()
        big.append(copy)
    own = pltpu.make_async_copy(cal_ref.at[mod], spot, l_sem.at[1])
    own.start()

    for copy in first:
        copy.wait()
    own_ref.wait()
    mine = pl.ds(pl.multiple_of(j * 128, 128), 128)
    for i in range(8):
        rtmp[4 * i:4 * i + 4, :] = ra[i, :, mine].astype(F32)
    rsl[...] = rtmp[...].astype(BF16)

    second = []
    for i in range(1, 8):
        copy = remote(rsl, rb.at[z], z_send.at[i - 1], z_recv.at[i - 1], device((z + i) % 8, y, x, core))
        copy.start()
        second.append(copy)
    own_z = pltpu.make_async_copy(rsl, rb.at[z], l_sem.at[0])
    own_z.start()

    s0.wait()
    shc_ref[...] = srow[...] + srow_in[...]
    sx[pl.ds(x, 1)] = shc_ref[...].reshape(1, 2, 128)
    s1 = []
    for i in range(1, 4):
        copy = remote(sx.at[x], sx.at[x], s_send.at[i], s_recv.at[i], device(z, y, (x + i) % 4, core))
        copy.start()
        s1.append(copy)

    for copy in second:
        copy.wait()
    own_z.wait()
    yrow = (y % 2) * 2 + y // 2
    third = []
    for i in range(1, 4):
        copy = remote(rb, rc.at[:, yrow], y_send.at[i - 1], y_recv.at[i - 1], device(z, (y + i) % 4, x, core))
        copy.start()
        third.append(copy)
    own_y = pltpu.make_async_copy(rb, rc.at[:, yrow], l_sem.at[0])
    own_y.start()

    for copy in s1:
        copy.wait()
    s2 = []
    for i in range(1, 4):
        copy = remote(sx, sy.at[y], s_send.at[3 + i], s_recv.at[3 + i], device(z, (y + i) % 4, x, core))
        copy.start()
        s2.append(copy)
    own_s = pltpu.make_async_copy(sx, sy.at[y], l_sem.at[2])
    own_s.start()

    for copy in third:
        copy.wait()
    own_y.wait()
    fourth = remote(rc.at[pl.ds(3 * (1 - core), 5)], rf_ref.at[x, core], c_send, c_recv, partner)
    fourth.start()
    own_c = pltpu.make_async_copy(rc.at[pl.ds(3 * core, 5)], rf_ref.at[x, core], l_sem.at[0])
    own_c.start()

    for copy in s2:
        copy.wait()
    own_s.wait()
    s3 = []
    for i in range(1, 8):
        copy = remote(sy, sha_ref.at[z], s_send.at[6 + i], s_recv.at[6 + i], device((z + i) % 8, y, x, core))
        copy.start()
        s3.append(copy)
    own_s2 = pltpu.make_async_copy(sy, sha_ref.at[z], l_sem.at[2])
    own_s2.start()

    fourth.wait()
    own_c.wait()
    fifth = []
    for i in range(1, 4):
        copy = remote(rf_ref.at[x], rf_ref.at[x], x_send.at[i - 1], x_recv.at[i - 1], device(z, y, (x + i) % 4, core))
        copy.start()
        fifth.append(copy)

    for copy in s3:
        copy.wait()
    own_s2.wait()
    for copy in fifth:
        copy.wait()
    for copy in big:
        copy.wait()
    own.wait()


def exchange(cal, ref, sh):
    dma = pltpu.SemaphoreType.DMA
    return pl.pallas_call(
        exchange_kernel,
        in_specs=[ANY, VM, VM],
        out_specs=[ANY, VM, VM, VM],
        out_shape=[
            jax.ShapeDtypeStruct((IMG, IMG), BF16),
            jax.ShapeDtypeStruct((4, 2, 5, 4, 32, 128), BF16),
            jax.ShapeDtypeStruct((2, 128), I32),
            jax.ShapeDtypeStruct((8, 4, 4, 2, 128), I32),
        ],
        scratch_shapes=[
            pltpu.VMEM((8, 4, IMG), BF16),
            pltpu.VMEM((32, 128), F32),
            pltpu.VMEM((32, 128), BF16),
            pltpu.VMEM((8, 32, 128), BF16),
            pltpu.VMEM((8, 4, 32, 128), BF16),
            pltpu.VMEM((2, 128), I32),
            pltpu.VMEM((2, 128), I32),
            pltpu.VMEM((4, 2, 128), I32),
            pltpu.VMEM((4, 4, 2, 128), I32),
            dma((15,)), dma((15,)), dma((7,)), dma((7,)), dma((7,)), dma((7,)), dma((3,)), dma((3,)),
            dma(()), dma(()), dma((3,)), dma((3,)), dma((14,)), dma((14,)), dma((3,)),
        ],
        compiler_params=pltpu.CompilerParams(collective_id=0, has_side_effects=True),
        name="exchange",
    )(cal, ref, sh)


def swap_kernel(rm_ref, out_ref, send, recv, sem):
    z, y, x, core = coords()
    partner = device(z, y, x, 1 - core)
    greet([partner])
    give = pl.ds(pl.multiple_of((1 - core) * 512, 512), 512)
    keep = pl.ds(pl.multiple_of(core * 512, 512), 512)
    copy = remote(rm_ref.at[give], out_ref.at[core], send, recv, partner)
    copy.start()
    own = pltpu.make_async_copy(rm_ref.at[keep], out_ref.at[core], sem)
    own.start()
    copy.wait()
    own.wait()


def swap(rm):
    dma = pltpu.SemaphoreType.DMA
    return pl.pallas_call(
        swap_kernel,
        in_specs=[VM],
        out_specs=VM,
        out_shape=jax.ShapeDtypeStruct((2, 512, IMG), BF16),
        scratch_shapes=[dma(()), dma(()), dma(())],
        compiler_params=pltpu.CompilerParams(collective_id=1, has_side_effects=True),
        name="swap",
    )(rm)


RROWS = 704
SROWS = 576


def track_kernel(core_ref, sh_ref, lab_ref, rf_ref, main_ref, halo_ref, row_ref, r3, held, part, wts, sp):
    core = core_ref[0]
    zero = jnp.zeros((RROWS, 128), F32)
    r3[0] = zero
    r3[9] = zero
    for b in range(8):
        r3[b + 1, 0:32, :] = jnp.zeros((32, 128), F32)
        r3[b + 1, 32:672, :] = rf_ref[b // 2, b % 2].reshape(640, 128).astype(F32)
        r3[b + 1, 672:704, :] = jnp.zeros((32, 128), F32)
    for b in range(10):
        sp[b] = jnp.zeros((SROWS, 128), F32)
    lane = lax.broadcasted_iota(I32, (TS, 128), 1)

    def place(t):
        g = t // 32
        ty = (t // 8) % 4
        tx = t % 8
        col = g * 64 + core * 32 + t % 32
        dy = sh_ref[0, col]
        dx = sh_ref[1, col]
        back = jnp.where(dx < 0, 1, 0).astype(I32)
        return g, ty, tx, dy, dx + 128 * back, tx + 1 - back

    def score_step(t, carry):
        g, ty, tx, dy, turn, block = place(t)
        tile = lab_ref[g, pl.ds(pl.multiple_of(ty * TS, TS), TS), pl.ds(pl.multiple_of(tx * 128, 128), 128)]
        tile = pltpu.roll(tile.astype(F32), turn, 1)
        held[t] = tile
        top = core * 128 + 32 + ty * TS + dy
        near = r3[block, pl.ds(top, TS), :]
        far = r3[block + 1, pl.ds(top, TS), :]
        product = tile * jnp.where(lane >= turn, near, far)
        part[t] = jnp.sum(product.reshape(16, 8, 128), axis=0)
        return carry

    lax.fori_loop(0, 64, score_step, 0)
    sums = jnp.sum(part[...], axis=1)
    score = jnp.broadcast_to(jnp.sum(sums, axis=1, keepdims=True) / TS, (64, 128))
    wts[...] = 1.0 / (1.0 + jnp.exp(-score))
    t_of = lax.broadcasted_iota(I32, (64, 128), 0)
    l_of = lax.broadcasted_iota(I32, (64, 128), 1)
    hit = l_of == (t_of // 32) * 64 + core * 32 + t_of % 32
    row_ref[...] = jnp.sum(jnp.where(hit, score, 0.0), axis=0, keepdims=True)

    def splat_step(t, carry):
        g, ty, tx, dy, turn, block = place(t)
        value = held[t] * wts[pl.ds(t, 1), :]
        top = 32 + ty * TS + dy
        sp[block, pl.ds(top, TS), :] += jnp.where(lane >= turn, value, 0.0)
        sp[block + 1, pl.ds(top, TS), :] += jnp.where(lane >= turn, 0.0, value)
        return carry

    lax.fori_loop(0, 64, splat_step, 0)
    edge = pl.multiple_of((1 - core) * 544, 32)
    for b in range(8):
        main_ref[b] = sp[b + 1, 32:544, :]
        halo_ref[b] = sp[b + 1, pl.ds(edge, 32), :]


def track(core, shc, lab, rf):
    return pl.pallas_call(
        track_kernel,
        in_specs=[
            pl.BlockSpec(memory_space=pltpu.SMEM),
            pl.BlockSpec(memory_space=pltpu.SMEM),
            VM,
            VM,
        ],
        out_specs=[VM, VM, VM],
        out_shape=[
            jax.ShapeDtypeStruct((8, 512, 128), F32),
            jax.ShapeDtypeStruct((8, 32, 128), F32),
            jax.ShapeDtypeStruct((1, 128), F32),
        ],
        scratch_shapes=[
            pltpu.VMEM((10, RROWS, 128), F32),
            pltpu.VMEM((64, TS, 128), F32),
            pltpu.VMEM((64, 8, 128), F32),
            pltpu.VMEM((64, 128), F32),
            pltpu.VMEM((10, SROWS, 128), F32),
        ],
        name="track",
    )(core, shc, lab, rf)


def ring_start(piece, me, right, left, fwd_a, fwd_b, fin_l, fin_r, send, recv):
    copies = [
        remote(piece((me + 2) % 4, 0), fwd_a, send.at[0], recv.at[0], right),
        remote(piece((me + 2) % 4, 1), fwd_b, send.at[1], recv.at[1], left),
        remote(piece((me + 1) % 4, 1), fin_l.at[1], send.at[2], recv.at[2], right),
        remote(piece((me + 3) % 4, 0), fin_r.at[0], send.at[3], recv.at[3], left),
    ]
    for copy in copies:
        copy.start()
    return copies


def ring_pass(piece, me, right, left, fwd_a, fwd_b, fin_l, fin_r, sum_a, sum_b, send, recv, copies):
    copies[0].wait_recv()
    sum_a[...] = fwd_a[...] + piece((me + 1) % 4, 0)[...]
    onward_a = remote(sum_a, fin_l.at[0], send.at[4], recv.at[4], right)
    onward_a.start()
    copies[1].wait_recv()
    sum_b[...] = fwd_b[...] + piece((me + 3) % 4, 1)[...]
    onward_b = remote(sum_b, fin_r.at[1], send.at[5], recv.at[5], left)
    onward_b.start()
    return copies + [onward_a, onward_b]


def ring_end(copies):
    for n, copy in enumerate(copies):
        copy.wait_send()
        if n >= 2:
            copy.wait_recv()


def finish_kernel(
    main_ref, halo_ref, row_ref, sha_ref, ref_ref,
    out_ref, score_ref,
    acc, halo_in, row_in, wx, wy, wz, smat, dmat, wmat, lhs, cov, unit, p_fwd, p_fin, p_sum, q_fwd, q_fin, q_sum, mid_p, mid_q,
    p2_fwd, p2_fin, p2_sum, q2_fwd, q2_fin, q2_sum, zout, zin,
    h_send, h_recv, w_send, w_recv, p_send, p_recv, q_send, q_recv, p2_send, p2_recv, q2_send, q2_recv,
    z_send, z_recv, l_sem,
):
    z, y, x, core = coords()
    partner = device(z, y, x, 1 - core)
    xs = [device(z, y, (x + i) % 4, core) for i in range(1, 4)]
    ys = [device(z, (y + i) % 4, x, core) for i in range(1, 4)]
    zs = [device((z + i) % 8, y, x, core) for i in range(1, 8)]
    zo = [device((z + i) % 8, y, x, 1 - core) for i in range(1, 8)]
    greet([partner] + xs + ys + zs + zo)

    halo = remote(halo_ref, halo_in, h_send, h_recv, partner)
    halo.start()
    row = remote(row_ref, row_in, w_send.at[0], w_recv.at[0], partner)
    row.start()
    acc[...] = main_ref[...].reshape(acc.shape)
    halo.wait()
    edge = 3 - 3 * core
    yl = 1 - core
    for b in range(8):
        acc[b, edge, yl, yl] += halo_in[b].reshape(4, 8, 128)

    def piece_px(d, half):
        return acc.at[pl.ds(2 * half, 2), :, :, :, d]

    def piece_qy(d, half):
        return acc.at[pl.ds(4 + 2 * half, 2), :, d % 2, d // 2]

    xr, xl = xs[0], xs[2]
    yr, yl_dev = ys[0], ys[2]
    args_p = (piece_px, x, xr, xl, p_fwd.at[0], p_fwd.at[1], p_fin.at[0], p_fin.at[1])
    args_q = (piece_qy, y, yr, yl_dev, q_fwd.at[0], q_fwd.at[1], q_fin.at[0], q_fin.at[1])
    cp = ring_start(*args_p, p_send, p_recv)
    cq = ring_start(*args_q, q_send, q_recv)

    row.wait()
    chip = row_ref[...] + row_in[...]
    both = jnp.where(core == 0, chip[:, 0:64], chip[:, 64:128])
    score_ref[...] = both
    wx[pl.ds(x, 1)] = chip.reshape(1, 1, 128)
    w1 = []
    for i in range(3):
        copy = remote(wx.at[x], wx.at[x], w_send.at[1 + i], w_recv.at[1 + i], xs[i])
        copy.start()
        w1.append(copy)

    cp = ring_pass(*args_p, p_sum.at[0], p_sum.at[1], p_send, p_recv, cp)
    cq = ring_pass(*args_q, q_sum.at[0], q_sum.at[1], q_send, q_recv, cq)

    for copy in w1:
        copy.wait()
    w2 = []
    for i in range(3):
        copy = remote(wx, wy.at[y], w_send.at[4 + i], w_recv.at[4 + i], ys[i])
        copy.start()
        w2.append(copy)
    own_w = pltpu.make_async_copy(wx, wy.at[y], l_sem.at[0])
    own_w.start()

    gather_rows(sha_ref, 0, smat)
    gather_rows(sha_ref, 1, dmat)
    smat[...] = jnp.transpose(smat[...])
    lane = lax.broadcasted_iota(I32, (128, 128), 1)
    for k in range(3):
        ty = jnp.clip(z - 1 + k, 0, 7)
        for g in range(2):
            moved = pltpu.roll(dmat[...], (128 - (g * 64 + ty * 8)) % 128, 1)
            for tx in range(8):
                dx = jnp.broadcast_to(moved[:, tx:tx + 1], (128, 128))
                edge_hit = jnp.where(lane < 64, jnp.where(lane < dx, 1.0, 0.0), jnp.where(lane >= 128 + dx, 1.0, 0.0))
                edge_hit = jnp.where(lane == 63, 1.0, edge_hit)
                unit[tx, pl.ds((2 * k + g) * 128, 128), :] = edge_hit.astype(BF16)

    for copy in w2:
        copy.wait()
    own_w.wait()
    w3 = []
    for i in range(7):
        copy = remote(wy, wz.at[z], w_send.at[7 + i], w_recv.at[7 + i], zs[i])
        copy.start()
        w3.append(copy)
    own_w2 = pltpu.make_async_copy(wy, wz.at[z], l_sem.at[0])
    own_w2.start()

    ring_end(cp)
    for h in range(2):
        mid_p[pl.ds(2 * h, 2)] = piece_px(x, h)[...] + p_fin[0, h] + p_fin[1, h]

    def piece_py(d, half):
        return mid_p.at[pl.ds(2 * half, 2), :, d % 2, d // 2]

    args_p2 = (piece_py, y, yr, yl_dev, p2_fwd.at[0], p2_fwd.at[1], p2_fin.at[0], p2_fin.at[1])
    cp2 = ring_start(*args_p2, p2_send, p2_recv)
    ring_end(cq)
    for h in range(2):
        mid_q[pl.ds(2 * h, 2)] = piece_qy(y, h)[...] + q_fin[0, h] + q_fin[1, h]

    def piece_qx(d, half):
        return mid_q.at[pl.ds(2 * half, 2), :, d]

    args_q2 = (piece_qx, x, xr, xl, q2_fwd.at[0], q2_fwd.at[1], q2_fin.at[0], q2_fin.at[1])
    cq2 = ring_start(*args_q2, q2_send, q2_recv)
    cp2 = ring_pass(*args_p2, p2_sum.at[0], p2_sum.at[1], p2_send, p2_recv, cp2)
    cq2 = ring_pass(*args_q2, q2_sum.at[0], q2_sum.at[1], q2_send, q2_recv, cq2)
    ring_end(cp2)
    ring_end(cq2)
    for h in range(2):
        got_p = piece_py(y, h)[...] + p2_fin[0, h] + p2_fin[1, h]
        got_q = piece_qx(x, h)[...] + q2_fin[0, h] + q2_fin[1, h]
        for b in range(2):
            for d in range(4):
                zout[d, 0, 2 * h + b] = got_p[b, d, 0:4, :]
                zout[d, 1, 2 * h + b] = got_p[b, d, 4:8, :]
                zout[d, 0, 4 + 2 * h + b] = got_q[b, d, 0:4, :]
                zout[d, 1, 4 + 2 * h + b] = got_q[b, d, 4:8, :]

    for d in range(4):
        for c in range(2):
            target_z = 4 * core + d
            self_hit = jnp.logical_and(target_z == z, core == c)

            @pl.when(jnp.logical_not(self_hit))
            def _():
                remote(zout.at[d, c], zin.at[z], z_send.at[d, c], z_recv.at[z], device(target_z, y, x, c)).start()

            @pl.when(self_hit)
            def _():
                pltpu.make_async_copy(zout.at[d, c], zin.at[z], l_sem.at[1]).start()

    for copy in w3:
        copy.wait()
    own_w2.wait()
    gather_rows(wz, 0, wmat)
    wmat[...] = jnp.transpose(1.0 / (1.0 + jnp.exp(-wmat[...])))
    r0 = z * 128 + (y % 2) * 64 + (y // 2) * 32 + x * 8 + core * 4
    for k in range(3):
        ty = jnp.clip(z - 1 + k, 0, 7)
        valid = jnp.where(ty == z - 1 + k, 1.0, 0.0).astype(F32)
        for g in range(2):
            rows = pl.ds(pl.multiple_of(g * 64 + ty * 8, 8), 8)
            low = smat[rows, :] + (ty * 128).astype(F32)
            w = wmat[rows, :] * valid
            w1 = w.astype(BF16).astype(F32)
            w2 = (w - w1).astype(BF16).astype(F32)
            w3 = w - w1 - w2
            cols = slice((2 * k + g) * 128, (2 * k + g + 1) * 128)
            for i in range(4):
                r = (r0 + i).astype(F32)
                hit = jnp.logical_and(low <= r, r < low + 128.0)
                for n, part in enumerate((w1, w2, w3)):
                    lhs[n * 4 + i, :, cols] = jnp.where(hit, part, 0.0)
    left = lhs[...].reshape(96, 768).astype(BF16)
    sub = lax.broadcasted_iota(I32, (12, 8, 128), 1)
    found = jnp.zeros((12, 8, 128), F32)
    for tx in range(8):
        product = jnp.dot(left, unit[tx], preferred_element_type=F32).reshape(12, 8, 128)
        found = jnp.where(sub == tx, product, found)
    found = found[0:4] + found[4:8] + found[8:12]
    tx_of = lax.broadcasted_iota(I32, (8, 128), 0)
    l_of = lax.broadcasted_iota(I32, (8, 128), 1)
    for i in range(4):
        total = jnp.sum(jnp.where(l_of == 63, found[i], 0.0), axis=1, keepdims=True)
        side = jnp.where(l_of == 63, 0.0, found[i])
        before = jnp.where(tx_of == 0, 0.0, pltpu.roll(side, 1, 0))
        after = jnp.where(tx_of == 7, 0.0, pltpu.roll(side, 7, 0))
        cover = total - side + jnp.where(l_of < 64, before, after)
        for b in range(8):
            cov[b, i:i + 1, :] = cover[b:b + 1, :]

    for d in range(4):
        for c in range(2):
            target_z = 4 * core + d
            self_hit = jnp.logical_and(target_z == z, core == c)

            @pl.when(jnp.logical_not(self_hit))
            def _():
                remote(zout.at[d, c], zin.at[z], z_send.at[d, c], z_recv.at[z], device(target_z, y, x, c)).wait_send()

    for s in range(8):
        self_hit = jnp.logical_and(z == s, core == z // 4)

        @pl.when(jnp.logical_not(self_hit))
        def _():
            remote(zout.at[0, 0], zin.at[s], z_send.at[0, 0], z_recv.at[s], partner).wait_recv()

        @pl.when(self_hit)
        def _():
            pltpu.make_async_copy(zout.at[0, 0], zin.at[s], l_sem.at[1]).wait()

    own_ref = ref_ref[...].astype(F32)
    for b in range(8):
        total = zin[0, b]
        for s in range(1, 8):
            total = total + zin[s, b]
        cols = slice(128 * b, 128 * b + 128)
        out_ref[:, cols] = (total + PRIOR * own_ref[:, cols]) / (cov[b] + PRIOR)


def gather_rows(source, which, target):
    def step(i, carry):
        target[pl.ds(i, 1), :] = source[i // 16, (i // 4) % 4, i % 4, which:which + 1, :].astype(target.dtype)
        return carry

    lax.fori_loop(0, 128, step, 0)


def finish(main, halo, row, sha, ref):
    dma = pltpu.SemaphoreType.DMA
    vm = pltpu.VMEM
    return pl.pallas_call(
        finish_kernel,
        in_specs=[VM, VM, VM, VM, VM],
        out_specs=[VM, VM],
        out_shape=[
            jax.ShapeDtypeStruct((4, IMG), F32),
            jax.ShapeDtypeStruct((1, 64), F32),
        ],
        scratch_shapes=[
            vm((8, 4, 2, 2, 4, 8, 128), F32),
            vm((8, 32, 128), F32),
            vm((1, 128), F32),
            vm((4, 1, 128), F32),
            vm((4, 4, 1, 128), F32),
            vm((8, 4, 4, 1, 128), F32),
            vm((128, 128), F32),
            vm((128, 128), I32),
            vm((128, 128), F32),
            vm((12, 8, 768), F32),
            vm((8, 4, 128), F32),
            vm((8, 768, 128), BF16),
            vm((2, 2, 4, 2, 2, 8, 128), F32),
            vm((2, 2, 2, 4, 2, 2, 8, 128), F32),
            vm((2, 2, 4, 2, 2, 8, 128), F32),
            vm((2, 2, 4, 4, 8, 128), F32),
            vm((2, 2, 2, 4, 4, 8, 128), F32),
            vm((2, 2, 4, 4, 8, 128), F32),
            vm((4, 4, 2, 2, 8, 128), F32),
            vm((4, 4, 4, 8, 128), F32),
            vm((2, 2, 4, 8, 128), F32),
            vm((2, 2, 2, 4, 8, 128), F32),
            vm((2, 2, 4, 8, 128), F32),
            vm((2, 2, 4, 8, 128), F32),
            vm((2, 2, 2, 4, 8, 128), F32),
            vm((2, 2, 4, 8, 128), F32),
            vm((4, 2, 8, 4, 128), F32),
            vm((8, 8, 4, 128), F32),
            dma(()), dma(()), dma((14,)), dma((14,)),
            dma((6,)), dma((6,)), dma((6,)), dma((6,)), dma((6,)), dma((6,)), dma((6,)), dma((6,)),
            dma((4, 2)), dma((8,)), dma((2,)),
        ],
        compiler_params=pltpu.CompilerParams(collective_id=2, has_side_effects=True),
        name="finish",
    )(main, halo, row, sha, ref)


def per_device(raw_frames, gain_section, offset, gain_factor, row_map, column_map, reference_image, shifts):
    cal = calibrate(raw_frames.reshape(16, MR, MC), gain_section.reshape(16, MR // 8, MC), offset[0], gain_factor[0])
    image, rf, shc, sha = exchange(cal, reference_image, shifts.reshape(2, 64))
    row_mapped = jnp.dot(row_map, image, preferred_element_type=F32).astype(BF16)
    halves = swap(row_mapped)
    lab = jnp.dot(halves.reshape(IMG, IMG), column_map, preferred_element_type=F32).astype(BF16)
    core = (lax.axis_index("pulse") % 2).astype(I32).reshape(1)
    main, halo, row = track(core, shc, lab.reshape(2, 512, IMG), rf)
    new_reference, scores = finish(main, halo, row, sha, reference_image)
    return scores.reshape(1, 1, TILES), new_reference


def solution(mesh):
    return jax.shard_map(
        per_device,
        mesh=mesh,
        in_specs=(
            P("pulse", None, "mod", None, None),
            P("pulse", None, "mod", None, None),
            P("mod", None, None, None),
            P("mod", None, None, None),
            P(),
            P(),
            P(("mod", "pulse"), None),
            P(None, "pulse", "mod", None),
        ),
        out_specs=(P("pulse", "mod", None), P(("mod", "pulse"), None)),
        check_vma=False,
    )
```

time: 1830 us -> 164 us (0.09)
  blocking collectives: 684 us -> 0 us
  waiting for transfers between devices: 409 us -> 0 us
  local copies, waits for them, and re-layouts: 307 us -> 2.45 us
  other arithmetic: 227 us -> 0 us
  Pallas kernels: 0 us -> 150 us
  loops' own time: 132 us -> 0 us
  matrix products: 32.6 us -> 11.1 us
    all_gather x2 -> x0, blocking collectives: 684 us -> none  [the longest x1 344 us: recount(): lax.all_gather(shift_rows.astype(jnp.float32), ('mod', 'pulse'), axis=0,...]
    all_gather x1 -> x0, waiting for transfers between devices: 361 us -> none  [per_device(): lax.all_gather(reference_image, ('mod', 'pulse'), axis=0, tiled=True)]
    dynamic_update_slice x64 -> x0, local copies, waits for them, and re-layouts: 205 us -> none  [tile_step(): lax.dynamic_update_slice(splat_map, current + weight * frame_tile, (top_e...]
    pallas_call x0 -> x5, Pallas kernels: none -> 150 us  [the longest x1 86 us: exchange(): pl.pallas_call(exchange_kernel, in_specs=[ANY, VM, VM], out_specs=[ANY, V...]
    another operation x2 -> x0, loops' own time: 132 us -> none  [the longest x1 131 us: track_tiles(): return lax.fori_loop(0, tiles_count, tile_step, start)]
    reduce_sum x64 -> x0, other arithmetic: 102 us -> none  [tile_step(): score_value = jnp.sum(frame_tile * window) / TS]
    dynamic_slice x136 -> x0, local copies, waits for them, and re-layouts: 75.1 us -> none  [the longest x64 37.7 us: tile_step(): top_edge = row_start + shift_rows[index] + SH]
    add x82 -> x0, other arithmetic: 65.3 us -> none  [the longest x64 65 us: tile_step(): current + weight * frame_tile]
  transfers between devices with their start and end apart: 3 -> 0, of which waited for: 2 -> 0; matrix products, arithmetic and copies ran while one was open for 1% -> 0% of each run, Pallas kernels for 0% -> 0%
where the time goes in v1:
time: 164 us
  Pallas kernels  150 us (91%)
  matrix products  11.1 us (7%)
  local copies, waits for them, and re-layouts  2.45 us (1%)
    pallas_call x1, Pallas kernels, exchange(): pl.pallas_call(exchange_kernel, in_specs=[ANY, VM, VM], out_specs=[ANY, V...  86 us
    pallas_call x1, Pallas kernels, finish(): pl.pallas_call(finish_kernel, in_specs=[VM, VM, VM, VM, VM], out_specs=[V...  34.1 us
    pallas_call x1, Pallas kernels, track(): pl.pallas_call(track_kernel, in_specs=[pl.BlockSpec(memory_space=pltpu.SM...  12.5 us
    pallas_call x1, Pallas kernels, calibrate(): pl.pallas_call(calibrate_kernel, grid=(frames,), in_specs=[pl.BlockSpec((...  11 us
    pallas_call x1, Pallas kernels, swap(): pl.pallas_call(swap_kernel, in_specs=[VM], out_specs=VM, out_shape=jax.Sh...  5.96 us
    dot_general x1, matrix products, per_device(): jnp.dot(halves.reshape(IMG, IMG), column_map, preferred_element_type=F32)  5.86 us
    dot_general x1, matrix products, per_device(): jnp.dot(row_map, image, preferred_element_type=F32).astype(BF16)  5.23 us

profile of v1, /device:TPU:1, one launch (start us, length us, event | category | flops | bytes accessed | tf_op | source)
XLA Modules:
  0.0 163.9 jit_solution(12888486806726153365)
XLA Ops:
  0.6 0.0 copy-start
  0.7 11.0 %calibrate.1.cal_ref = bf16[16,128,512]{2,1,0:T(8,128)(2,1)} custom-call(bf16[16,128,512]{2,1,0:T(8,128)(2,1)} %bitcast.15, s32[16,16,512]{2,1,0:T(8,128)} %bitcast.20, f32[3,128,512]{2,1,0:T(8,128)} %bitcast.18, f32[3,128,512]{2,1,0:T(8,128)} %bitcast.19), custom_call_target="tpu_custom_call" | custom-call | tf_op jit(solution)/shard_map/calibrate/pallas_call | solution.py:80
  11.7 86.0 %exchange.1 = (bf16[1024,1024]{1,0:T(8,128)(2,1)}, bf16[4,2,5,4,32,128]{5,4,3,2,1,0:T(8,128)(2,1)}, s32[2,128]{1,0:T(2,128)}, s32[8,4,4,2,128]{4,3,2,1,0:T(2,128)}) custom-call(bf16[16,128,512]{2,1,0:T(8,128)(2,1)} %calibrate.1.cal_ref, bf16[4,1024]{1,0:T(4,128)(2,1)} %ref_ref.3, s32[2,64]{1,0:T(2,128)} %bitcast.21), custom_call_target="tpu_custom_call" | custom-call | tf_op jit(solution)/shard_map/exchange/pallas_call | solution.py:225
  97.7 0.0 copy-done
  97.7 5.2 %convert_bitcast_fusion.rm_ref = bf16[1024,1024]{1,0:T(8,128)(2,1)} fusion(bf16[1024,1024]{1,0:T(8,128)(2,1)S(1)} %copy-done, bf16[1024,1024]{1,0:T(8,128)(2,1)} %get-tuple-element.12), kind=kOutput, calls=%fused_computation | convolution fusion | flops 2148532224 | bytes 6291456 | tf_op jit(solution)/shard_map/dot_general | solution.py:663
  102.9 6.0 %swap.1 = bf16[2,512,1024]{2,1,0:T(8,128)(2,1)} custom-call(bf16[1024,1024]{1,0:T(8,128)(2,1)} %convert_bitcast_fusion.rm_ref), custom_call_target="tpu_custom_call" | custom-call | tf_op jit(solution)/shard_map/swap/pallas_call | solution.py:269
  108.9 5.9 %convolution_convert_fusion = bf16[1024,1024]{1,0:T(8,128)(2,1)} fusion(bf16[1024,1024]{1,0:T(8,128)(2,1)} %bitcast.17, bf16[1024,1024]{1,0:T(8,128)(2,1)} %param.13), kind=kOutput, calls=%fused_computation.1 | convolution fusion | flops 2148532224 | bytes 6291456 | tf_op jit(solution)/shard_map/dot_general | solution.py:665
  114.7 12.5 %track.1 = (f32[8,512,128]{2,1,0:T(8,128)}, f32[8,32,128]{2,1,0:T(8,128)}, f32[1,128]{1,0:T(1,128)}) custom-call(s32[1]{0:T(128)} %bitcast.core_ref, s32[2,128]{1,0:T(2,128)} %get-tuple-element.11.sh_ref, bf16[2,512,1024]{2,1,0:T(8,128)(2,1)} %bitcast.16, bf16[4,2,5,4,32,128]{5,4,3,2,1,0:T(8,128)(2,1)} %get-tuple-element.13.rf_ref), custom_call_target="tpu_custom_call" | custom-call | tf_op jit(solution)/shard_map/track/pallas_call | solution.py:344
  127.3 34.1 %finish.1 = (f32[4,1024]{1,0:T(4,128)}, f32[1,64]{1,0:T(1,128)}) custom-call(f32[8,512,128]{2,1,0:T(8,128)} %get-tuple-element.14.main_ref, f32[8,32,128]{2,1,0:T(8,128)} %get-tuple-element.15.halo_ref, f32[1,128]{1,0:T(1,128)} %get-tuple-element.16.row_ref, s32[8,4,4,2,128]{4,3,2,1,0:T(2,128)} %get-tuple-element.17.sha_ref, bf16[4,1024]{1,0:T(4,128)(2,1)} %ref_ref.3), custom_call_target="tpu_custom_call" | custom-call | tf_op jit(solution)/shard_map/finish/pallas_call | solution.py:614
  161.4 1.1 copy.14
  162.5 1.3 copy.15
Async XLA Ops:
  0.6 97.0 %copy-start = (bf16[1024,1024]{1,0:T(8,128)(2,1)S(1)}, bf16[1024,1024]{1,0:T(8,128)(2,1)}, u32[]{:S(2)}) copy-start(bf16[1024,1024]{1,0:T(8,128)(2,1)} %param.12) | copy-start | bytes 6291460

commit v2 on v1

--- a/solution.py
+++ b/solution.py
@@ -1,5 +1,3 @@
-import functools
-
 import jax
 import jax.numpy as jnp
 from jax import lax
@@ -56,60 +54,78 @@
 ANY = pl.BlockSpec(memory_space=pl.ANY)
 
 
-def calibrate_kernel(raw_ref, gain_ref, off_ref, fac_ref, out_ref):
+ORDER = (1, 7, 2, 6, 3, 5, 4)
+SENDS = [(dz, 0) for dz in ORDER] + [(dz, 1) for dz in ORDER] + [(0, 1)]
+
+
+def calibrate_frame(slot, raw, gain, off, fac, cal):
     k = lax.broadcasted_iota(I32, (8, MC), 0)
     inv = jnp.full((8, MC), 1.0, F32)
     for step in range(1, 8):
         inv = jnp.where(k == step, jnp.float32(1.0 / 3.0**step), inv)
     inv_next = inv * jnp.float32(1.0 / 3.0)
-    for p in range(MR // 8):
-        rows = pl.ds(8 * p, 8)
-        packed = gain_ref[0, pl.ds(p, 1), :].astype(F32) + 0.5
-        packed = jnp.broadcast_to(packed, (8, MC))
-        digit = jnp.floor(packed * inv) - 3.0 * jnp.floor(packed * inv_next)
+
+    def digits(row):
+        packed = jnp.broadcast_to(gain[slot, pl.ds(row, 1), :].astype(F32) + 0.5, (8, MC))
+        return jnp.floor(packed * inv) - 3.0 * jnp.floor(packed * inv_next)
+
+    def step(p, carry):
+        rows = pl.ds(pl.multiple_of(16 * p, 16), 16)
+        digit = jnp.concatenate([digits(2 * p), digits(2 * p + 1)], axis=0)
         low = digit < 0.5
         mid = digit < 1.5
-        dark = jnp.where(low, off_ref[0, rows, :], jnp.where(mid, off_ref[1, rows, :], off_ref[2, rows, :]))
-        fac = jnp.where(low, fac_ref[0, rows, :], jnp.where(mid, fac_ref[1, rows, :], fac_ref[2, rows, :]))
-        value = (raw_ref[0, rows, :].astype(F32) - dark) * fac
-        out_ref[0, rows, :] = value.astype(BF16)
-
-
-def calibrate(raw, gain, off, fac):
-    frames = raw.shape[0]
-    return pl.pallas_call(
-        calibrate_kernel,
-        grid=(frames,),
-        in_specs=[
-            pl.BlockSpec((1, MR, MC), lambda f: (f, 0, 0)),
-            pl.BlockSpec((1, MR // 8, MC), lambda f: (f, 0, 0)),
-            pl.BlockSpec((3, MR, MC), lambda f: (0, 0, 0)),
-            pl.BlockSpec((3, MR, MC), lambda f: (0, 0, 0)),
-        ],
-        out_specs=pl.BlockSpec((1, MR, MC), lambda f: (f, 0, 0)),
-        out_shape=jax.ShapeDtypeStruct((frames, MR, MC), BF16),
-        name="calibrate",
-    )(raw, gain, off, fac)
+        dark = jnp.where(low, off[0, rows, :], jnp.where(mid, off[1, rows, :], off[2, rows, :]))
+        scale = jnp.where(low, fac[0, rows, :], jnp.where(mid, fac[1, rows, :], fac[2, rows, :]))
+        cal[slot, rows, :] = ((raw[slot, rows, :].astype(F32) - dark) * scale).astype(BF16)
+        return carry
+
+    lax.fori_loop(0, 8, step, 0)
 
 
 def exchange_kernel(
-    cal_ref, ref_ref, sh_ref,
-    img_ref, rf_ref, shc_ref, sha_ref,
-    ra, rtmp, rsl, rb, rc, srow, srow_in, sx, sy,
-    a_send, a_recv, r_send, r_recv, z_send, z_recv, y_send, y_recv,
-    c_send, c_recv, x_send, x_recv, s_send, s_recv, l_sem,
+    raw_hbm, gain_hbm, off_hbm, fac_hbm, rmap_hbm, cmap_hbm, ref_ref, sh_ref,
+    lab_ref, rf_ref, shc_ref, sha_ref,
+    raw, gain, off, fac, rmap, cmap, cal, img, acc, rm_own, rm_out, rm_in,
+    ra, rtmp, rsl, rb, rc, srow, srow_in, sz, sy,
+    in_sem, raw_sem, a_send, a_recv, r_send, r_recv, z_send, z_recv, y_send, y_recv,
+    c_send, c_recv, x_send, x_recv, s_send, s_recv, m_send, m_recv, l_sem,
 ):
     z, y, x, core = coords()
-    mod = lax.axis_index("mod")
+    yl = y % 2
+    mod = z * 2 + yl
     pulse = lax.axis_index("pulse")
-    peers = [((mod + i) % 16, pulse) for i in range(1, 16)]
+    partner = device(z, y, x, 1 - core)
+
+    def goal(dz, dl):
+        return ((z + dz) % 8) * 2 + (yl + dl) % 2
+
+    loads = [
+        pltpu.make_async_copy(gain_hbm, gain, in_sem.at[0]),
+        pltpu.make_async_copy(off_hbm, off, in_sem.at[1]),
+        pltpu.make_async_copy(fac_hbm, fac, in_sem.at[2]),
+    ]
+    for copy in loads:
+        copy.start()
+    frames = SENDS + [(0, 0)]
+    raw_loads = []
+    for n, (dz, dl) in enumerate(frames):
+        t = goal(dz, dl)
+        copy = pltpu.make_async_copy(raw_hbm.at[t], raw.at[t], raw_sem.at[n])
+        copy.start()
+        raw_loads.append(copy)
+    maps = [
+        pltpu.make_async_copy(rmap_hbm, rmap, in_sem.at[3]),
+        pltpu.make_async_copy(cmap_hbm, cmap, in_sem.at[4]),
+    ]
+    for copy in maps:
+        copy.start()
+
     plane = [device(z, y, (x + (i // 2)) % 4, (core + i) % 2) for i in range(1, 8)]
-    greet(peers + plane + [device(z, (y + 2) % 4, x, core), device(z, (y + 3 - 2 * (y % 2)) % 4, x, core)])
-
-    quad = mod // 4
-    row0 = pl.multiple_of((quad // 2) * 512 + (mod % 4) * MR, MR)
-    col0 = pl.multiple_of((quad % 2) * MC, MC)
-    spot = img_ref.at[pl.ds(row0, MR), pl.ds(col0, MC)]
+    greet(
+        [(goal(dz, dl), pulse) for dz, dl in SENDS]
+        + plane
+        + [device(z, (y + 2) % 4, x, core), device(z, (y + 3 - 2 * yl) % 4, x, core)]
+    )
 
     j = x * 2 + core
     first = []
@@ -124,17 +140,26 @@
     srow[:, 0:64] = sh_ref[...]
     srow[:, 64:128] = sh_ref[...]
     srow[...] = jnp.where(lane // 64 == core, srow[...], 0)
-    partner = device(z, y, x, 1 - core)
     s0 = remote(srow, srow_in, s_send.at[0], s_recv.at[0], partner)
     s0.start()
 
+    for copy in loads:
+        copy.wait()
     big = []
-    for i in range(1, 16):
-        copy = remote(cal_ref.at[(mod + i) % 16], spot, a_send.at[i - 1], a_recv.at[i - 1], peers[i - 1])
+
+    def compute(n):
+        raw_loads[n].wait()
+        calibrate_frame(goal(*frames[n]), raw, gain, off, fac, cal)
+
+    def send(n):
+        t = goal(*SENDS[n])
+        spot = img.at[z, pl.ds(pl.multiple_of(yl * MR, MR), MR)]
+        copy = remote(cal.at[t], spot, a_send.at[n], a_recv.at[n], (t, pulse))
         copy.start()
         big.append(copy)
-    own = pltpu.make_async_copy(cal_ref.at[mod], spot, l_sem.at[1])
-    own.start()
+
+    compute(0)
+    compute(1)
 
     for copy in first:
         copy.wait()
@@ -143,7 +168,6 @@
     for i in range(8):
         rtmp[4 * i:4 * i + 4, :] = ra[i, :, mine].astype(F32)
     rsl[...] = rtmp[...].astype(BF16)
-
     second = []
     for i in range(1, 8):
         copy = remote(rsl, rb.at[z], z_send.at[i - 1], z_recv.at[i - 1], device((z + i) % 8, y, x, core))
@@ -151,20 +175,26 @@
         second.append(copy)
     own_z = pltpu.make_async_copy(rsl, rb.at[z], l_sem.at[0])
     own_z.start()
-
     s0.wait()
     shc_ref[...] = srow[...] + srow_in[...]
-    sx[pl.ds(x, 1)] = shc_ref[...].reshape(1, 2, 128)
     s1 = []
-    for i in range(1, 4):
-        copy = remote(sx.at[x], sx.at[x], s_send.at[i], s_recv.at[i], device(z, y, (x + i) % 4, core))
+    for i in range(1, 8):
+        copy = remote(shc_ref, sz.at[z], s_send.at[i], s_recv.at[i], device((z + i) % 8, y, x, core))
         copy.start()
         s1.append(copy)
+    own_s = pltpu.make_async_copy(shc_ref, sz.at[z], l_sem.at[2])
+    own_s.start()
+
+    send(0)
+    send(1)
+    for n in range(2, 7):
+        compute(n)
+        send(n)
 
     for copy in second:
         copy.wait()
     own_z.wait()
-    yrow = (y % 2) * 2 + y // 2
+    yrow = yl * 2 + y // 2
     third = []
     for i in range(1, 4):
         copy = remote(rb, rc.at[:, yrow], y_send.at[i - 1], y_recv.at[i - 1], device(z, (y + i) % 4, x, core))
@@ -172,16 +202,20 @@
         third.append(copy)
     own_y = pltpu.make_async_copy(rb, rc.at[:, yrow], l_sem.at[0])
     own_y.start()
-
     for copy in s1:
         copy.wait()
+    own_s.wait()
     s2 = []
     for i in range(1, 4):
-        copy = remote(sx, sy.at[y], s_send.at[3 + i], s_recv.at[3 + i], device(z, (y + i) % 4, x, core))
+        copy = remote(sz, sy.at[y], s_send.at[7 + i], s_recv.at[7 + i], device(z, (y + i) % 4, x, core))
         copy.start()
         s2.append(copy)
-    own_s = pltpu.make_async_copy(sx, sy.at[y], l_sem.at[2])
+    own_s = pltpu.make_async_copy(sz, sy.at[y], l_sem.at[2])
     own_s.start()
+
+    for n in range(7, 12):
+        compute(n)
+        send(n)
 
     for copy in third:
         copy.wait()
@@ -190,17 +224,20 @@
     fourth.start()
     own_c = pltpu.make_async_copy(rc.at[pl.ds(3 * core, 5)], rf_ref.at[x, core], l_sem.at[0])
     own_c.start()
-
     for copy in s2:
         copy.wait()
     own_s.wait()
     s3 = []
-    for i in range(1, 8):
-        copy = remote(sy, sha_ref.at[z], s_send.at[6 + i], s_recv.at[6 + i], device((z + i) % 8, y, x, core))
+    for i in range(1, 4):
+        copy = remote(sy, sha_ref.at[x], s_send.at[10 + i], s_recv.at[10 + i], device(z, y, (x + i) % 4, core))
         copy.start()
         s3.append(copy)
-    own_s2 = pltpu.make_async_copy(sy, sha_ref.at[z], l_sem.at[2])
-    own_s2.start()
+    own_s = pltpu.make_async_copy(sy, sha_ref.at[x], l_sem.at[2])
+    own_s.start()
+
+    for n in range(12, 15):
+        compute(n)
+        send(n)
 
     fourth.wait()
     own_c.wait()
@@ -210,71 +247,104 @@
         copy.start()
         fifth.append(copy)
 
+    compute(15)
+    own = pltpu.make_async_copy(cal.at[mod], img.at[z, pl.ds(pl.multiple_of(yl * MR, MR), MR)], l_sem.at[1])
+    own.start()
+    acc[...] = jnp.zeros_like(acc)
+    for copy in maps:
+        copy.wait()
+    own.wait()
+
+    def add_rows(zz):
+        half = (zz // 2) % 2
+        k0 = pl.multiple_of((zz // 4) * 512 + (zz % 2) * 256, 256)
+
+        def step(n, carry):
+            cols = pl.ds(pl.multiple_of(n * 256, 256), 256)
+            acc[half, :, cols] += jnp.dot(rmap[:, pl.ds(k0, 256)], img[zz, :, cols], preferred_element_type=F32)
+            return carry
+
+        lax.fori_loop(0, 2, step, 0)
+
+    big[14].wait_recv()
+    add_rows(z)
+    for n in range(7):
+        big[n].wait_recv()
+        big[7 + n].wait_recv()
+        add_rows((z + 8 - ORDER[n]) % 8)
+
+    give = pl.ds(pl.multiple_of((1 - core) * 512, 512), 512)
+    keep = pl.ds(pl.multiple_of(core * 512, 512), 512)
+    for h in range(2):
+        rm_out[:, 512 * h:512 * h + 512] = acc[h, give, :].astype(BF16)
+    swap = remote(rm_out, rm_in, m_send, m_recv, partner)
+    swap.start()
+    for h in range(2):
+        rm_own[:, 512 * h:512 * h + 512] = acc[h, keep, :].astype(BF16)
+
+    def columns(source, g):
+        def step(n, carry):
+            cols = pl.ds(pl.multiple_of(n * 256, 256), 256)
+            lab_ref[g, :, cols] = jnp.dot(source[...], cmap[:, cols], preferred_element_type=F32).astype(BF16)
+            return carry
+
+        lax.fori_loop(0, 4, step, 0)
+
+    columns(rm_own, core)
+    swap.wait()
+    columns(rm_in, 1 - core)
+
     for copy in s3:
         copy.wait()
-    own_s2.wait()
+    own_s.wait()
     for copy in fifth:
         copy.wait()
     for copy in big:
-        copy.wait()
-    own.wait()
-
-
-def exchange(cal, ref, sh):
+        copy.wait_send()
+
+
+def exchange(raw, gain, off, fac, rmap, cmap, ref, sh):
     dma = pltpu.SemaphoreType.DMA
+    vm = pltpu.VMEM
     return pl.pallas_call(
         exchange_kernel,
-        in_specs=[ANY, VM, VM],
-        out_specs=[ANY, VM, VM, VM],
+        in_specs=[ANY, ANY, ANY, ANY, ANY, ANY, VM, VM],
+        out_specs=[VM, VM, VM, VM],
         out_shape=[
-            jax.ShapeDtypeStruct((IMG, IMG), BF16),
+            jax.ShapeDtypeStruct((2, 512, IMG), BF16),
             jax.ShapeDtypeStruct((4, 2, 5, 4, 32, 128), BF16),
             jax.ShapeDtypeStruct((2, 128), I32),
-            jax.ShapeDtypeStruct((8, 4, 4, 2, 128), I32),
+            jax.ShapeDtypeStruct((4, 4, 8, 2, 128), I32),
         ],
         scratch_shapes=[
-            pltpu.VMEM((8, 4, IMG), BF16),
-            pltpu.VMEM((32, 128), F32),
-            pltpu.VMEM((32, 128), BF16),
-            pltpu.VMEM((8, 32, 128), BF16),
-            pltpu.VMEM((8, 4, 32, 128), BF16),
-            pltpu.VMEM((2, 128), I32),
-            pltpu.VMEM((2, 128), I32),
-            pltpu.VMEM((4, 2, 128), I32),
-            pltpu.VMEM((4, 4, 2, 128), I32),
+            vm((16, MR, MC), BF16),
+            vm((16, MR // 8, MC), I32),
+            vm((3, MR, MC), F32),
+            vm((3, MR, MC), F32),
+            vm((IMG, IMG), BF16),
+            vm((IMG, IMG), BF16),
+            vm((16, MR, MC), BF16),
+            vm((8, 256, 512), BF16),
+            vm((2, IMG, 512), F32),
+            vm((512, IMG), BF16),
+            vm((512, IMG), BF16),
+            vm((512, IMG), BF16),
+            vm((8, 4, IMG), BF16),
+            vm((32, 128), F32),
+            vm((32, 128), BF16),
+            vm((8, 32, 128), BF16),
+            vm((8, 4, 32, 128), BF16),
+            vm((2, 128), I32),
+            vm((2, 128), I32),
+            vm((8, 2, 128), I32),
+            vm((4, 8, 2, 128), I32),
+            dma((5,)), dma((16,)),
             dma((15,)), dma((15,)), dma((7,)), dma((7,)), dma((7,)), dma((7,)), dma((3,)), dma((3,)),
-            dma(()), dma(()), dma((3,)), dma((3,)), dma((14,)), dma((14,)), dma((3,)),
+            dma(()), dma(()), dma((3,)), dma((3,)), dma((14,)), dma((14,)), dma(()), dma(()), dma((3,)),
         ],
         compiler_params=pltpu.CompilerParams(collective_id=0, has_side_effects=True),
         name="exchange",
-    )(cal, ref, sh)
-
-
-def swap_kernel(rm_ref, out_ref, send, recv, sem):
-    z, y, x, core = coords()
-    partner = device(z, y, x, 1 - core)
-    greet([partner])
-    give = pl.ds(pl.multiple_of((1 - core) * 512, 512), 512)
-    keep = pl.ds(pl.multiple_of(core * 512, 512), 512)
-    copy = remote(rm_ref.at[give], out_ref.at[core], send, recv, partner)
-    copy.start()
-    own = pltpu.make_async_copy(rm_ref.at[keep], out_ref.at[core], sem)
-    own.start()
-    copy.wait()
-    own.wait()
-
-
-def swap(rm):
-    dma = pltpu.SemaphoreType.DMA
-    return pl.pallas_call(
-        swap_kernel,
-        in_specs=[VM],
-        out_specs=VM,
-        out_shape=jax.ShapeDtypeStruct((2, 512, IMG), BF16),
-        scratch_shapes=[dma(()), dma(()), dma(())],
-        compiler_params=pltpu.CompilerParams(collective_id=1, has_side_effects=True),
-        name="swap",
-    )(rm)
+    )(raw, gain, off, fac, rmap, cmap, ref, sh)
 
 
 RROWS = 704
@@ -400,7 +470,7 @@
 def finish_kernel(
     main_ref, halo_ref, row_ref, sha_ref, ref_ref,
     out_ref, score_ref,
-    acc, halo_in, row_in, wx, wy, wz, smat, dmat, wmat, lhs, cov, unit, p_fwd, p_fin, p_sum, q_fwd, q_fin, q_sum, mid_p, mid_q,
+    acc, halo_in, row_in, wr, wx, wy, wz, smat, dmat, wmat, lhs, cov, unit, p_fwd, p_fin, p_sum, q_fwd, q_fin, q_sum, mid_p, mid_q,
     p2_fwd, p2_fin, p2_sum, q2_fwd, q2_fin, q2_sum, zout, zin,
     h_send, h_recv, w_send, w_recv, p_send, p_recv, q_send, q_recv, p2_send, p2_recv, q2_send, q2_recv,
     z_send, z_recv, l_sem,
@@ -441,28 +511,31 @@
     chip = row_ref[...] + row_in[...]
     both = jnp.where(core == 0, chip[:, 0:64], chip[:, 64:128])
     score_ref[...] = both
-    wx[pl.ds(x, 1)] = chip.reshape(1, 1, 128)
+    wr[...] = chip
     w1 = []
-    for i in range(3):
-        copy = remote(wx.at[x], wx.at[x], w_send.at[1 + i], w_recv.at[1 + i], xs[i])
+    for i in range(7):
+        copy = remote(wr, wx.at[z], w_send.at[1 + i], w_recv.at[1 + i], zs[i])
         copy.start()
         w1.append(copy)
+    own_w = pltpu.make_async_copy(wr, wx.at[z], l_sem.at[0])
+    own_w.start()
 
     cp = ring_pass(*args_p, p_sum.at[0], p_sum.at[1], p_send, p_recv, cp)
     cq = ring_pass(*args_q, q_sum.at[0], q_sum.at[1], q_send, q_recv, cq)
 
     for copy in w1:
         copy.wait()
+    own_w.wait()
     w2 = []
     for i in range(3):
-        copy = remote(wx, wy.at[y], w_send.at[4 + i], w_recv.at[4 + i], ys[i])
+        copy = remote(wx, wy.at[y], w_send.at[8 + i], w_recv.at[8 + i], ys[i])
         copy.start()
         w2.append(copy)
     own_w = pltpu.make_async_copy(wx, wy.at[y], l_sem.at[0])
     own_w.start()
 
-    gather_rows(sha_ref, 0, smat)
-    gather_rows(sha_ref, 1, dmat)
+    gather_rows(sha_ref, 0, smat, 8)
+    gather_rows(sha_ref, 1, dmat, 8)
     smat[...] = jnp.transpose(smat[...])
     lane = lax.broadcasted_iota(I32, (128, 128), 1)
     for k in range(3):
@@ -479,11 +552,11 @@
         copy.wait()
     own_w.wait()
     w3 = []
-    for i in range(7):
-        copy = remote(wy, wz.at[z], w_send.at[7 + i], w_recv.at[7 + i], zs[i])
+    for i in range(3):
+        copy = remote(wy, wz.at[x], w_send.at[11 + i], w_recv.at[11 + i], xs[i])
         copy.start()
         w3.append(copy)
-    own_w2 = pltpu.make_async_copy(wy, wz.at[z], l_sem.at[0])
+    own_w2 = pltpu.make_async_copy(wy, wz.at[x], l_sem.at[0])
     own_w2.start()
 
     ring_end(cp)
@@ -534,7 +607,7 @@
     for copy in w3:
         copy.wait()
     own_w2.wait()
-    gather_rows(wz, 0, wmat)
+    gather_rows(wz, 0, wmat, 8)
     wmat[...] = jnp.transpose(1.0 / (1.0 + jnp.exp(-wmat[...])))
     r0 = z * 128 + (y % 2) * 64 + (y // 2) * 32 + x * 8 + core * 4
     for k in range(3):
@@ -600,9 +673,10 @@
         out_ref[:, cols] = (total + PRIOR * own_ref[:, cols]) / (cov[b] + PRIOR)
 
 
-def gather_rows(source, which, target):
+def gather_rows(source, which, target, inner):
     def step(i, carry):
-        target[pl.ds(i, 1), :] = source[i // 16, (i // 4) % 4, i % 4, which:which + 1, :].astype(target.dtype)
+        row = source[i // (4 * inner), (i // inner) % 4, i % inner, which:which + 1, :]
+        target[pl.ds(i, 1), :] = row.astype(target.dtype)
         return carry
 
     lax.fori_loop(0, 128, step, 0)
@@ -623,9 +697,10 @@
             vm((8, 4, 2, 2, 4, 8, 128), F32),
             vm((8, 32, 128), F32),
             vm((1, 128), F32),
-            vm((4, 1, 128), F32),
-            vm((4, 4, 1, 128), F32),
-            vm((8, 4, 4, 1, 128), F32),
+            vm((1, 128), F32),
+            vm((8, 1, 128), F32),
+            vm((4, 8, 1, 128), F32),
+            vm((4, 4, 8, 1, 128), F32),
             vm((128, 128), F32),
             vm((128, 128), I32),
             vm((128, 128), F32),
@@ -658,13 +733,18 @@
 
 
 def per_device(raw_frames, gain_section, offset, gain_factor, row_map, column_map, reference_image, shifts):
-    cal = calibrate(raw_frames.reshape(16, MR, MC), gain_section.reshape(16, MR // 8, MC), offset[0], gain_factor[0])
-    image, rf, shc, sha = exchange(cal, reference_image, shifts.reshape(2, 64))
-    row_mapped = jnp.dot(row_map, image, preferred_element_type=F32).astype(BF16)
-    halves = swap(row_mapped)
-    lab = jnp.dot(halves.reshape(IMG, IMG), column_map, preferred_element_type=F32).astype(BF16)
+    lab, rf, shc, sha = exchange(
+        raw_frames.reshape(16, MR, MC),
+        gain_section.reshape(16, MR // 8, MC),
+        offset[0],
+        gain_factor[0],
+        row_map,
+        column_map,
+        reference_image,
+        shifts.reshape(2, 64),
+    )
     core = (lax.axis_index("pulse") % 2).astype(I32).reshape(1)
-    main, halo, row = track(core, shc, lab.reshape(2, 512, IMG), rf)
+    main, halo, row = track(core, shc, lab, rf)
     new_reference, scores = finish(main, halo, row, sha, reference_image)
     return scores.reshape(1, 1, TILES), new_reference
 

time: 164 us -> 127 us (0.77)
  Pallas kernels: 150 us -> 123 us
  matrix products: 11.1 us -> 0 us
    pallas_call x3 -> x1, Pallas kernels: 103 us -> 73.4 us  [exchange(): pl.pallas_call(exchange_kernel, in_specs=[ANY, ANY, ANY, ANY, ANY, ANY, V...]
    dot_general x2 -> x0, matrix products: 11.1 us -> none  [the longest x1 5.86 us: per_device(): jnp.dot(halves.reshape(IMG, IMG), column_map, preferred_element_type=F32)]
    pallas_call x1, Pallas kernels: 34.1 us -> 37.3 us  [finish(): pl.pallas_call(finish_kernel, in_specs=[VM, VM, VM, VM, VM], out_specs=[V...]
where the time goes in v2:
time: 127 us; the launch traced here: 126 us
  Pallas kernels  123 us (97%)
  local copies, waits for them, and re-layouts  2.49 us (2%)
    pallas_call x1, Pallas kernels, exchange(): pl.pallas_call(exchange_kernel, in_specs=[ANY, ANY, ANY, ANY, ANY, ANY, V...  73.4 us
    pallas_call x1, Pallas kernels, finish(): pl.pallas_call(finish_kernel, in_specs=[VM, VM, VM, VM, VM], out_specs=[V...  37.3 us
    pallas_call x1, Pallas kernels, track(): pl.pallas_call(track_kernel, in_specs=[pl.BlockSpec(memory_space=pltpu.SM...  12.5 us

profile of v2, /device:TPU:1, one launch (start us, length us, event | category | flops | bytes accessed | tf_op | source)
XLA Modules:
  0.0 126.4 jit_solution(2846047043632003643)
XLA Ops:
  0.6 73.4 %exchange.1 = (bf16[2,512,1024]{2,1,0:T(8,128)(2,1)}, bf16[4,2,5,4,32,128]{5,4,3,2,1,0:T(8,128)(2,1)}, s32[2,128]{1,0:T(2,128)}, s32[4,4,8,2,128]{4,3,2,1,0:T(2,128)}) custom-call(bf16[16,128,512]{2,1,0:T(8,128)(2,1)} %bitcast.7, s32[16,16,512]{2,1,0:T(8,128)} %bitcast.10, f32[3,128,512]{2,1,0:T(8,128)} %bitcast.8, f32[3,128,512]{2,1,0:T(8,128)} %bitcast.9, ...), custom_call_target="tpu_custom_call" | custom-call | tf_op jit(solution)/shard_map/exchange/pallas_call | solution.py:309
  74.0 12.5 %track.1 = (f32[8,512,128]{2,1,0:T(8,128)}, f32[8,32,128]{2,1,0:T(8,128)}, f32[1,128]{1,0:T(1,128)}) custom-call(s32[1]{0:T(128)} %bitcast.core_ref, s32[2,128]{1,0:T(2,128)} %get-tuple-element.11.sh_ref, bf16[2,512,1024]{2,1,0:T(8,128)(2,1)} %get-tuple-element.12.lab_ref, bf16[4,2,5,4,32,128]{5,4,3,2,1,0:T(8,128)(2,1)} %get-tuple-element.13.rf_ref), custom_call_target="tpu_custom_call" | custom-call | tf_op jit(solution)/shard_map/track/pallas_call | solution.py:414
  86.6 37.3 %finish.1 = (f32[4,1024]{1,0:T(4,128)}, f32[1,64]{1,0:T(1,128)}) custom-call(f32[8,512,128]{2,1,0:T(8,128)} %get-tuple-element.14.main_ref, f32[8,32,128]{2,1,0:T(8,128)} %get-tuple-element.15.halo_ref, f32[1,128]{1,0:T(1,128)} %get-tuple-element.16.row_ref, s32[4,4,8,2,128]{4,3,2,1,0:T(2,128)} %get-tuple-element.17.sha_ref, bf16[4,1024]{1,0:T(4,128)(2,1)} %ref_ref.3), custom_call_target="tpu_custom_call" | custom-call | tf_op jit(solution)/shard_map/finish/pallas_call | solution.py:688
  123.9 1.2 copy.12
  125.0 1.3 %copy.13 = f32[4,1024]{1,0:T(4,128)} copy(f32[4,1024]{1,0:T(4,128)} %get-tuple-element.23) | data formatting | bytes 32768
